TPU v7x, 512 devices: a whole 4x4x16 slice. The times are simulated.
512 devices in a mesh: gx: 16 (over x, y_lo, core), gy: 32 (over y_hi, z).
Axes of the slice: x: 4, y: 4 (y_hi: 2, y_lo: 2; y = y_hi * 2 + y_lo), z: 16, core: 2. Of those that a mesh axis runs over, the one named last changes fastest.
Arguments:
- plate_motion: bfloat16 [32, 64, 128, 2, 128], P('gx', 'gy'), may hold values from -6 to 6
- adjoint_load: bfloat16 [32, 64, 128, 2, 128], P('gx', 'gy'), may hold values from -6 to 6
- excitation: bfloat16 [32, 64, 128, 2, 128], P('gx', 'gy'), may hold values from -6 to 6
- coupling: bfloat16 [32, 64, 5, 2, 128, 128], P('gx', 'gy'), may hold values from -0.25 to 0.25
- joints: int32 [32, 64, 4], P('gx', 'gy'), may hold values 0 or 1
- hydro: bfloat16 [2, 16384, 16384], P(None, 'gx', 'gy'), may hold values from -0.046875 to 0.046875
- panel_map: bfloat16 [16384, 2, 2, 128], P(('gx', 'gy')), may hold values from -0.25 to 0.25
Outputs:
- residual: float32 [32, 64, 128, 2, 128], P('gx', 'gy')
- multiplier: float32 [32, 64, 128, 2, 128], P('gx', 'gy')
- sensitivity: float32 [32, 64], P('gx', 'gy')
All inputs are finite; a program needn't handle non-finite values. No bound on the sum of `joints` on one device may be relied on, other than what follows from the above.
Results may differ from a plain program's by a relative error of at most 0.0031.
Values may be sent and summed in bfloat16 or wider, within the bound.
A program may use at most 64 MiB of HBM per device.

v0:
```python
import math

import jax
import jax.numpy as jnp
from jax import lax
from jax.sharding import PartitionSpec as P


def extended(x, sides, width):
    for axis, dim in sides:
        size, length = (lax.axis_size(axis), x.shape[dim])
        up = [(i, (i + 1) % size) for i in range(size - 1)]
        down = [(j, i) for i, j in up]
        last = lax.slice_in_dim(x, length - width, length, axis=dim)
        first = lax.slice_in_dim(x, 0, width, axis=dim)
        before = lax.ppermute(last, axis, up)
        after = lax.ppermute(first, axis, down)
        x = jnp.concatenate([before, x, after], axis=dim)
    return x


def complex_apply(form, coupling, vector):
    real_c = coupling[..., 0, :, :]
    imag_c = coupling[..., 1, :, :]
    real_v = vector[..., 0, :]
    imag_v = vector[..., 1, :]

    def mult(matrix, values):
        return jnp.einsum(form, matrix, values, preferred_element_type=jnp.float32)

    return jnp.stack(
        [mult(real_c, real_v) - mult(imag_c, imag_v), mult(real_c, imag_v) + mult(imag_c, real_v)],
        axis=-2,
    )


def adjoint_apply(form, coupling, vector):
    real_c = coupling[..., 0, :, :]
    imag_c = coupling[..., 1, :, :]
    real_v = vector[..., 0, :]
    imag_v = vector[..., 1, :]

    def mult(matrix, values):
        return jnp.einsum(form, matrix, values, preferred_element_type=jnp.float32)

    return jnp.stack(
        [mult(real_c, real_v) + mult(imag_c, imag_v), mult(real_c, imag_v) - mult(imag_c, real_v)],
        axis=-2,
    )


def plain_product(matrix, values):
    return jnp.dot(matrix, values, preferred_element_type=jnp.float32)


def flipped_product(matrix, values):
    return lax.dot_general(
        matrix, values, (((0,), (0,)), ((), ())), preferred_element_type=jnp.float32
    )


def on_device(plate_motion, adjoint_load, excitation, coupling, joints, hydro, panel_map):
    rows_count = plate_motion.shape[0]
    cols_count = plate_motion.shape[1]
    panel_count = panel_map.shape[0]
    unknowns = plate_motion.shape[4]
    cases = plate_motion.shape[2]
    links = joints.astype(jnp.float32)[:, :, :, None, None, None]
    padded = extended(plate_motion, (("gx", 0), ("gy", 1)), 1)
    beside_all = jnp.stack(
        [
            padded[0:rows_count, 1:-1],
            padded[2:, 1:-1],
            padded[1:-1, 0:cols_count],
            padded[1:-1, 2:],
        ],
        axis=2,
    )
    own = complex_apply("xyij,xyhj->xyhi", coupling[:, :, 0], plate_motion)
    structural = own + jnp.sum(
        links * complex_apply("xydij,xydhj->xydhi", coupling[:, :, 1:], beside_all), axis=2
    )
    outgoing = links * adjoint_apply("xydji,xyhj->xydhi", coupling[:, :, 1:], adjoint_load)
    own_adjoint = adjoint_apply("xyji,xyhj->xyhi", coupling[:, :, 0], adjoint_load)
    layered = extended(outgoing, (("gx", 0), ("gy", 1)), 1)
    incoming = (
        layered[2:, 1:-1, 0] + layered[:-2, 1:-1, 1] + layered[1:-1, 2:, 2] + layered[1:-1, :-2, 3]
    )
    lift = math.sqrt(rows_count * cols_count * unknowns / panel_count)
    motion_panels = jnp.einsum(
        "nxyk,xyhck->cnh", panel_map, plate_motion, preferred_element_type=jnp.float32
    ).astype(jnp.bfloat16)
    load_panels = jnp.einsum(
        "nxyk,xyhck->cnh", panel_map, adjoint_load, preferred_element_type=jnp.float32
    ).astype(jnp.bfloat16)
    piece = lax.all_gather(motion_panels, "gx", axis=1, tiled=True)
    first = plain_product(hydro[0], piece[0]) - plain_product(hydro[1], piece[1])
    second = plain_product(hydro[0], piece[1]) + plain_product(hydro[1], piece[0])
    pressure_part = jnp.stack([first, second])
    piece = lax.all_gather(load_panels, "gy", axis=1, tiled=True)
    first = flipped_product(hydro[0], piece[0]) + flipped_product(hydro[1], piece[1])
    second = flipped_product(hydro[0], piece[1]) - flipped_product(hydro[1], piece[0])
    reaction_part = jnp.stack([first, second])
    pressure_band = lax.psum(pressure_part, "gy")
    pressure = lax.dynamic_slice_in_dim(
        pressure_band, lax.axis_index("gy") * panel_count, panel_count, 1
    )
    reaction_band = lax.psum(reaction_part, "gx")
    reaction = lax.dynamic_slice_in_dim(
        reaction_band, lax.axis_index("gx") * panel_count, panel_count, 1
    )
    pressure = pressure.astype(jnp.bfloat16)
    reaction = reaction.astype(jnp.bfloat16)
    pressure_force = jnp.einsum(
        "nxyk,cnh->xyhck", panel_map, pressure, preferred_element_type=jnp.float32
    )
    reaction_force = jnp.einsum(
        "nxyk,cnh->xyhck", panel_map, reaction, preferred_element_type=jnp.float32
    )
    residual = structural + lift * pressure_force - excitation.astype(jnp.float32)
    multiplier = own_adjoint + incoming + lift * reaction_force
    sensitivity = jnp.sum(multiplier * own, axis=(2, 3, 4)) / math.sqrt(cases * unknowns)
    return (residual, multiplier, sensitivity)


def solution(mesh):
    placed = (
        P("gx", "gy", None, None, None),
        P("gx", "gy", None, None, None),
        P("gx", "gy", None, None, None),
        P("gx", "gy", None, None, None, None),
        P("gx", "gy", None),
        P(None, "gx", "gy"),
        P(("gx", "gy"), None, None, None),
    )
    return jax.shard_map(
        on_device,
        mesh=mesh,
        in_specs=placed,
        out_specs=(P("gx", "gy", None, None, None), P("gx", "gy", None, None, None), P("gx", "gy")),
        check_vma=False,
    )
```

profile of v0, /device:TPU:14, one launch (start us, length us, event | category | flops | bytes accessed | tf_op | source)
XLA Modules:
  0.0 440.0 jit_solution(6919222201309677431)
XLA Ops:
  0.6 1.0 copy.43
  1.7 0.7 fusion.106
  2.4 1.9 collective-permute-start
  4.3 3.6 collective-permute-start.1
  8.0 1.3 slice_bitcast_fusion.2
  9.4 1.3 fusion.59
  10.9 1.0 copy_bitcast_fusion
  12.1 84.5 %all_gather.7 = bf16[2,1024,128]{2,1,0:T(8,128)(2,1)S(1)} all-gather(bf16[2,32,128]{2,1,0:T(8,128)(2,1)S(1)} %fusion.19), channel_id=1, replica_groups=mesh['gx'=16,'gy'=32] {'gy'}, dimensions={1}, use_global_device_ids=true | all-gather | bytes 540672 | tf_op jit(solution)/shard_map/all_gather | solution.py:100
  96.6 1.2 fusion.25
  97.9 1.2 fusion.27
  99.3 16.8 %all_gather.6 = bf16[2,512,128]{2,1,0:T(8,128)(2,1)S(1)} all-gather(bf16[2,32,128]{2,1,0:T(8,128)(2,1)S(1)} %fusion.20), channel_id=1, replica_groups=mesh['gx'=16,'gy'=32] {'gx'}, dimensions={1}, use_global_device_ids=true | all-gather | bytes 278528 | tf_op jit(solution)/shard_map/all_gather | solution.py:96
  116.2 1.2 fusion.29
  117.4 1.2 fusion.31
  118.9 2.0 fusion.15
  120.9 1.6 fusion.16
  122.6 0.4 fusion.5
  123.0 0.4 fusion.6
  123.5 0.3 copy-done
  124.4 0.6 copy-done.5
  125.1 0.9 constant_dynamic-update-slice_fusion
  126.1 1.3 collective-permute-start.2
  127.4 1.3 collective-permute-start.3
  128.7 1.1 pad_maximum_fusion.2
  129.9 0.9 fusion.66
  130.8 2.9 collective-permute-done.2
  133.7 4.1 collective-permute-done.3
  138.1 0.5 fusion.51
  138.6 0.5 fusion.47
  139.1 0.5 fusion.4
  139.6 0.5 fusion.3
  140.1 1.3 maximum_multiply_fusion.1
  141.3 1.6 fusion.104
  142.9 1.9 collective-permute-start.4
  144.8 3.4 collective-permute-start.5
  148.2 0.8 pad_maximum_fusion.12
  149.4 0.9 fusion.12
  150.7 18.0 %collective-permute-done.4 = f32[1,2,4,128,2,128]{5,3,1,0,4,2:T(8,128)} collective-permute-done((f32[1,2,4,128,2,128]{5,3,1,0,4,2:T(8,128)}, f32[1,2,4,128,2,128]{5,3,1,0,4,2:T(8,128)}, u32[]{:S(2)}, u32[]{:S(2)}) %collective-permute-start.4) | collective-permute-done | bytes 1048608 | tf_op jit(solution)/shard_map/ppermute | solution.py:17
  168.7 2.0 pad_maximum_fusion
  170.7 2.5 fusion.103
  173.2 1.4 collective-permute-start.6
  174.6 5.9 %collective-permute-start.7 = (f32[4,1,4,128,2,128]{5,3,1,0,4,2:T(8,128)}, f32[4,1,4,128,2,128]{5,3,1,0,4,2:T(8,128)}, u32[]{:S(2)}, u32[]{:S(2)}) collective-permute-start(f32[4,1,4,128,2,128]{5,3,1,0,4,2:T(8,128)} %get-tuple-element.10), channel_id=1, source_target_pairs={{0,1},{1,2},{2,3},{3,4},{4,5},{5,6},{6,7},{7,8},{8,9},{9,10},{10,1... | collective-permute-start | bytes 6291464 | tf_op jit(solution)/shard_map/ppermute | solution.py:16
  181.0 98.1 %all-reduce.2 = bf16[2,512,128]{2,1,0:T(8,128)(2,1)} all-reduce(f32[2,512,128]{2,1,0:T(8,128)} %pad_maximum_fusion.12), channel_id=1, replica_groups=mesh['gx'=16,'gy'=32] {'gx'}, use_global_device_ids=true, to_apply=%region_2.0 | all-reduce | flops 131072 | bytes 786432 | tf_op jit(solution)/shard_map/psum | solution.py:108
  279.1 154.9 %all-reduce.3 = bf16[2,1024,128]{2,1,0:T(8,128)(2,1)} all-reduce(f32[2,1024,128]{2,1,0:T(8,128)} %pad_maximum_fusion.2), channel_id=1, replica_groups=mesh['gx'=16,'gy'=32] {'gy'}, use_global_device_ids=true, to_apply=%region_1.0 | all-reduce | flops 262144 | bytes 1572864 | tf_op jit(solution)/shard_map/psum | solution.py:104
  434.0 1.4 fusion.10
  435.4 1.2 copy.80
  436.6 1.6 multiply_reduce_fusion
  438.2 1.2 copy.81
  439.4 0.6 broadcast_multiply_fusion
  (50 shorter events, 3.1 us)
Async XLA Ops:
  0.6 8.6 %copy-start.9 = (bf16[2,2,128,2,128]{4,3,2,1,0:T(2,128)(2,1)S(1)}, bf16[2,2,128,2,128]{4,3,2,1,0:T(2,128)(2,1)}, u32[]{:S(2)}) copy-start(bf16[2,2,128,2,128]{4,3,2,1,0:T(2,128)(2,1)} %param.8) | copy-start | bytes 786436
  2.4 122.0 %collective-permute-start = (bf16[1,2,128,2,128]{4,2,1,0,3:T(8,128)(2,1)}, bf16[1,2,128,2,128]{4,2,1,0,3:T(8,128)(2,1)S(1)}, u32[]{:S(2)}, u32[]{:S(2)}) collective-permute-start(bf16[1,2,128,2,128]{4,2,1,0,3:T(8,128)(2,1)} %get-tuple-element.24), channel_id=1, source_target_pairs={{0,32},{32,64},{64,96},{96,128},{128,160},{160,192},{192,224},{224... | collective-permute-start | bytes 393224 | tf_op jit(solution)/shard_map/ppermute | solution.py:16
  4.3 120.8 %collective-permute-start.1 = (bf16[1,2,128,2,128]{4,2,1,0,3:T(8,128)(2,1)}, bf16[1,2,128,2,128]{4,2,1,0,3:T(8,128)(2,1)}, u32[]{:S(2)}, u32[]{:S(2)}) collective-permute-start(bf16[1,2,128,2,128]{4,2,1,0,3:T(8,128)(2,1)} %get-tuple-element.23), channel_id=1, source_target_pairs={{32,0},{64,32},{96,64},{128,96},{160,128},{192,160},{224,192},{256... | collective-permute-start | bytes 393224 | tf_op jit(solution)/shard_map/ppermute | solution.py:17
  9.3 2.6 copy-start.10
  9.3 87.3 %copy-start.1 = (bf16[2,1024,512]{2,1,0:T(8,128)(2,1)S(1)}, bf16[2,1024,512]{2,1,0:T(8,128)(2,1)}, u32[]{:S(2)}) copy-start(bf16[2,1024,512]{2,1,0:T(8,128)(2,1)} %param.12) | copy-start | bytes 6291460
  12.1 87.0 %copy-start.4 = (bf16[2,2,128,2,128]{4,3,2,1,0:T(2,128)(2,1)S(1)}, bf16[2,2,128,2,128]{4,3,2,1,0:T(2,128)(2,1)}, u32[]{:S(2)}) copy-start(bf16[2,2,128,2,128]{4,3,2,1,0:T(2,128)(2,1)} %param.7) | copy-start | bytes 786436
  96.6 19.5 %copy-start.8 = (bf16[2,1024,128]{2,1,0:T(8,128)(2,1)}, bf16[2,1024,128]{2,1,0:T(8,128)(2,1)S(1)}, u32[]{:S(2)}) copy-start(bf16[2,1024,128]{2,1,0:T(8,128)(2,1)S(1)} %all_gather.7) | copy-start | bytes 1572868
  99.1 19.5 %copy-start.12 = (s32[2,2,4]{2,1,0:T(2,128)S(1)}, s32[2,2,4]{2,1,0:T(2,128)}, u32[]{:S(2)}) copy-start(s32[2,2,4]{2,1,0:T(2,128)} %param.11) | copy-start | bytes 196
  118.7 2.2 copy-start.2
  118.7 3.8 copy-start.7
  120.9 2.1 copy-start.6
  122.6 1.2 copy-start
  124.1 1.0 copy-start.5
  126.1 7.6 %collective-permute-start.2 = (bf16[4,1,128,2,128]{4,2,1,0,3:T(8,128)(2,1)S(1)}, bf16[4,1,128,2,128]{4,2,1,0,3:T(8,128)(2,1)S(1)}, u32[]{:S(2)}, u32[]{:S(2)}) collective-permute-start(bf16[4,1,128,2,128]{4,2,1,0,3:T(8,128)(2,1)S(1)} %get-tuple-element.19), channel_id=1, source_target_pairs={{0,1},{1,2},{2,3},{3,4},{4,5},{5,6},{6,7},{7,8},{8,9},{9,10},{10,1... | collective-permute-start | bytes 786440 | tf_op jit(solution)/shard_map/ppermute | solution.py:16
  127.4 10.4 %collective-permute-start.3 = (bf16[4,1,128,2,128]{4,2,1,0,3:T(8,128)(2,1)S(1)}, bf16[4,1,128,2,128]{4,2,1,0,3:T(8,128)(2,1)S(1)}, u32[]{:S(2)}, u32[]{:S(2)}) collective-permute-start(bf16[4,1,128,2,128]{4,2,1,0,3:T(8,128)(2,1)S(1)} %get-tuple-element.20), channel_id=1, source_target_pairs={{1,0},{2,1},{3,2},{4,3},{5,4},{6,5},{7,6},{8,7},{9,8},{10,9},{11,1... | collective-permute-start | bytes 786440 | tf_op jit(solution)/shard_map/ppermute | solution.py:17
  142.9 25.8 %collective-permute-start.4 = (f32[1,2,4,128,2,128]{5,3,1,0,4,2:T(8,128)}, f32[1,2,4,128,2,128]{5,3,1,0,4,2:T(8,128)}, u32[]{:S(2)}, u32[]{:S(2)}) collective-permute-start(f32[1,2,4,128,2,128]{5,3,1,0,4,2:T(8,128)} %get-tuple-element.12), channel_id=1, source_target_pairs={{32,0},{64,32},{96,64},{128,96},{160,128},{192,160},{224,192},{256... | collective-permute-start | bytes 3145736 | tf_op jit(solution)/shard_map/ppermute | solution.py:17
  144.8 23.8 %collective-permute-start.5 = (f32[1,2,4,128,2,128]{5,3,1,0,4,2:T(8,128)}, f32[1,2,4,128,2,128]{5,3,1,0,4,2:T(8,128)}, u32[]{:S(2)}, u32[]{:S(2)}) collective-permute-start(f32[1,2,4,128,2,128]{5,3,1,0,4,2:T(8,128)} %get-tuple-element.11), channel_id=1, source_target_pairs={{0,32},{32,64},{64,96},{96,128},{128,160},{160,192},{192,224},{224... | collective-permute-start | bytes 3145736 | tf_op jit(solution)/shard_map/ppermute | solution.py:16
  173.2 260.8 %copy-start.11 = (bf16[32,2,2,128]{3,2,1,0:T(2,128)(2,1)S(1)}, bf16[32,2,2,128]{3,2,1,0:T(2,128)(2,1)}, u32[]{:S(2)}) copy-start(bf16[32,2,2,128]{3,2,1,0:T(2,128)(2,1)} %param.13) | copy-start | bytes 98308
  173.2 263.4 %collective-permute-start.6 = (f32[4,1,4,128,2,128]{5,3,1,0,4,2:T(8,128)}, f32[4,1,4,128,2,128]{5,3,1,0,4,2:T(8,128)}, u32[]{:S(2)}, u32[]{:S(2)}) collective-permute-start(f32[4,1,4,128,2,128]{5,3,1,0,4,2:T(8,128)} %get-tuple-element.9), channel_id=1, source_target_pairs={{1,0},{2,1},{3,2},{4,3},{5,4},{6,5},{7,6},{8,7},{9,8},{10,9},{11,1... | collective-permute-start | bytes 6291464 | tf_op jit(solution)/shard_map/ppermute | solution.py:17
  174.6 262.0 %collective-permute-start.7 = (f32[4,1,4,128,2,128]{5,3,1,0,4,2:T(8,128)}, f32[4,1,4,128,2,128]{5,3,1,0,4,2:T(8,128)}, u32[]{:S(2)}, u32[]{:S(2)}) collective-permute-start(f32[4,1,4,128,2,128]{5,3,1,0,4,2:T(8,128)} %get-tuple-element.10), channel_id=1, source_target_pairs={{0,1},{1,2},{2,3},{3,4},{4,5},{5,6},{6,7},{7,8},{8,9},{9,10},{10,1... | collective-permute-start | bytes 6291464 | tf_op jit(solution)/shard_map/ppermute | solution.py:16
  434.0 2.7 copy-start.3
where the time goes:
time: 441 us; the launch traced here: 440 us
  blocking collectives  354 us (80%)
  waiting for transfers between devices  25.1 us (6%)
  starting transfers between devices  20.7 us (5%)
  matrix products  19 us (4%)
  local copies, waits for them, and re-layouts  12.8 us (3%)
  other arithmetic  6.95 us (2%)
    psum x1, blocking collectives, on_device(): pressure_band = lax.psum(pressure_part, 'gy')  155 us
    psum x1, blocking collectives, on_device(): reaction_band = lax.psum(reaction_part, 'gx')  98.1 us
    all_gather x1, blocking collectives, on_device(): piece = lax.all_gather(load_panels, 'gy', axis=1, tiled=True)  84.5 us
    ppermute x4, waiting for transfers between devices, extended(): after = lax.ppermute(first, axis, down)  22.1 us
    all_gather x1, blocking collectives, on_device(): piece = lax.all_gather(motion_panels, 'gx', axis=1, tiled=True)  16.8 us
    ppermute x4, starting transfers between devices, extended(): before = lax.ppermute(last, axis, up)  12.5 us
  transfers between devices with their start and end apart: 8, of which 3 were waited for; matrix products, arithmetic and copies ran while one was open for 5% of the time, Pallas kernels for 0%

commit v1 on v0

v1 whole, which is shorter than its diff:
```python
import functools
import math

import jax
import jax.numpy as jnp
from jax import lax
from jax.experimental import pallas as pl
from jax.experimental.pallas import tpu as pltpu
from jax.sharding import PartitionSpec as P

MESH = pl.DeviceIdType.MESH
F32 = jnp.float32
BF16 = jnp.bfloat16
NGX, NGY, NZ = 16, 32, 16
PD = 32
FAR = 5
CHUNKS = (0, FAR, NZ - FAR)


def nn(a, b):
    return jnp.dot(a, b, preferred_element_type=F32)


def nt(a, b):
    return lax.dot_general(a, b, (((1,), (1,)), ((), ())), preferred_element_type=F32)


def tn(a, b):
    return lax.dot_general(a, b, (((0,), (0,)), ((), ())), preferred_element_type=F32)


def times_i(x):
    rows = x.shape[0]
    even = lax.rem(lax.broadcasted_iota(jnp.int32, x.shape, 0), 2) == 0
    return jnp.where(even, -pltpu.roll(x, rows - 1, 0), pltpu.roll(x, 1, 0))


def lane_i(width):
    r = lax.broadcasted_iota(jnp.int32, (width, width), 0)
    c = lax.broadcasted_iota(jnp.int32, (width, width), 1)
    odd = lax.rem(c, 2) == 1
    plus = jnp.where(jnp.logical_and(odd, r == c - 1), 1.0, 0.0)
    minus = jnp.where(jnp.logical_and(jnp.logical_not(odd), r == c + 1), 1.0, 0.0)
    return (plus - minus).astype(BF16)


def kernel(
    joints, plate_h, adj_h, exc_h, coup_h, hyd_h, pmap_h,
    res_h, mult_h, own_h, pressure_o, reaction_o, map_o,
    X, A, JA, E, C, H, HT, PM, PM32, MG, MP, LG, LP, PO, PB, YB, SB, RA, TB, RB, QB, RG,
    HX, HY, TX, TY, RX, RY, RES, MULT, OWN,
    lsem, gx_s, gx_r, fa_s, fa_r, nb_s, nb_r, yf_s, yf_r, yx_s, yx_r,
    ra_s, ra_r, rb_s, rb_r, rx_s, rx_r, h_s, h_r,
):
    gx = lax.axis_index("gx")
    gy = lax.axis_index("gy")
    yh = lax.div(gy, NZ)
    z = lax.rem(gy, NZ)

    def gx_at(r):
        return lax.rem(gx + r, NGX)

    def gy_at(dz, dy):
        return lax.rem(yh + dy, 2) * NZ + lax.rem(z + dz, NZ)

    def near(q):
        return lax.rem(lax.rem(q + 2, 5) - 2 + NZ, NZ)

    def each(lo, hi, f):
        def body(i, carry):
            f(i)
            return carry
        lax.fori_loop(lo, hi, body, 0)

    def remote(src, dst, send, recv, where):
        return pltpu.make_async_remote_copy(
            src, dst, send, recv, device_id=where, device_id_type=MESH)

    loads = [
        pltpu.make_async_copy(s, d, lsem.at[i])
        for i, (s, d) in enumerate(
            ((pmap_h, PM), (adj_h, A), (plate_h, X), (coup_h, C), (hyd_h, H), (exc_h, E))
        )
    ]
    for c in loads:
        c.start()

    bar = pltpu.get_barrier_semaphore()

    def greet(x, y):
        pl.semaphore_signal(bar, inc=1, device_id=(x, y), device_id_type=MESH)

    for dz in (FAR, NZ - FAR, 3, NZ - 3):
        greet(gx, gy_at(dz, 0))
    greet(gx, gy_at(0, 1))
    for step in (1, NGY - 1):
        greet(gx, lax.rem(gy + step, NGY))
    each(1, 5, lambda q: greet(gx, gy_at(near(q), 0)))
    each(1, NGX, lambda r: greet(gx_at(r), gy))

    def far_gather(i):
        return remote(LG.at[gy], LG.at[gy], fa_s.at[i], fa_r.at[i],
                      (gx, gy_at((FAR, NZ - FAR)[i], 0)))

    def far_gather_in(i):
        slot = gy_at((NZ - FAR, FAR)[i], 0)
        return remote(LG.at[slot], LG.at[slot], fa_s.at[i], fa_r.at[i], (gx, slot))

    def gather(r):
        return remote(MG.at[gx], MG.at[gx], gx_s.at[r], gx_r.at[r], (gx_at(r), gy))

    def gather_in(r):
        slot = gx_at(NGX - r)
        return remote(MG.at[slot], MG.at[slot], gx_s.at[r], gx_r.at[r], (slot, gy))

    def near_gather(q, c):
        slot = gy_at(CHUNKS[c], 0)
        return remote(LG.at[slot], LG.at[slot], nb_s.at[q, c], nb_r.at[q, c],
                      (gx, gy_at(near(q), 0)))

    def near_slot(q, c):
        return lax.rem(NZ - near(q) + CHUNKS[c], NZ)

    def near_gather_in(q, c):
        slot = gy_at(near_slot(q, c), 0)
        return remote(LG.at[slot], LG.at[slot], nb_s.at[q, c], nb_r.at[q, c], (gx, slot))

    def opposite_gather():
        slot = gy_at(NZ - FAR, 0)
        return remote(LG.at[slot], LG.at[slot], nb_s.at[0, 0], nb_r.at[0, 0], (gx, gy_at(3, 0)))

    def opposite_gather_in():
        slot = gy_at(8, 0)
        return remote(LG.at[slot], LG.at[slot], nb_s.at[0, 0], nb_r.at[0, 0], (gx, slot))

    def across(o):
        slot = gy_at(o, 0)
        return remote(LG.at[slot], LG.at[slot], yf_s.at[o], yf_r.at[o], (gx, gy_at(0, 1)))

    def across_in(o):
        slot = gy_at(o, 1)
        return remote(LG.at[slot], LG.at[slot], yf_s.at[o], yf_r.at[o], (gx, gy_at(0, 1)))

    def swap(t):
        rows = pl.ds(t * 8, 8)
        return remote(PB.at[rows], YB.at[rows], yx_s.at[t], yx_r.at[t], (gx, gy_at(0, 1)))

    def near_part(q, c):
        return remote(SB.at[lax.rem(z + near(q) + CHUNKS[c], NZ)], RA.at[q, c],
                      ra_s.at[q, c], ra_r.at[q, c], (gx, gy_at(near(q), 0)))

    def opposite_part():
        return remote(SB.at[lax.rem(z + 8, NZ)], RA.at[0, 0],
                      ra_s.at[0, 0], ra_r.at[0, 0], (gx, gy_at(3, 0)))

    def far_part(i):
        return remote(TB.at[i], RB.at[i], rb_s.at[i], rb_r.at[i],
                      (gx, gy_at((FAR, NZ - FAR)[i], 0)))

    def sum_part(r):
        return remote(QB.at[gx_at(r)], RG.at[r], rx_s.at[r], rx_r.at[r], (gx_at(r), gy))

    def halo_x(src, dst, k, s):
        return remote(src.at[s], dst.at[1 - s], h_s.at[k, s], h_r.at[k, 1 - s],
                      (gx_at(1 if s else NGX - 1), gy))

    def halo_y(src, dst, k, s):
        return remote(src.at[:, s] if k == 1 else src.at[s], dst.at[1 - s],
                      h_s.at[k, s], h_r.at[k, 1 - s],
                      (gx, lax.rem(gy + (1 if s else NGY - 1), NGY)))

    loads[0].wait()
    PM32[...] = PM[...].astype(F32)
    for b in range(4):
        map_o[:, b * 128:(b + 1) * 128] = PM32[pl.ds(b, PD, stride=4), :].astype(BF16)

    def panels(V):
        total = nt(map_o[:, 0:128], V[0, 0])
        for b in range(1, 4):
            total = total + nt(map_o[:, b * 128:(b + 1) * 128], V[b // 2, b % 2])
        return total.astype(BF16)

    loads[1].wait()
    LG[gy] = panels(A)
    loads[2].wait()
    MG[gx] = panels(X)

    pl.semaphore_wait(bar, 4 + 1 + 2 + 4 + 15)

    for i in range(2):
        far_gather(i).start()
    each(1, NGX, lambda r: gather(r).start())
    across(0).start()
    each(1, 5, lambda q: near_gather(q, 0).start())

    loads[3].wait()

    def link(bx, by, d):
        return joints[bx, by, d].astype(F32)

    def edge_x(bx):
        v = gx + 2 * bx - 1
        return jnp.where(jnp.logical_and(v >= 0, v < NGX), 1.0, 0.0).astype(F32)

    def edge_y(by):
        v = gy + 2 * by - 1
        return jnp.where(jnp.logical_and(v >= 0, v < NGY), 1.0, 0.0).astype(F32)

    def back(bx, by, d):
        m = (bx * 2 + by) * 5 + d
        return nn(A[bx, by], C[m, 0]) - nn(JA[bx, by], C[m, 1])

    def outgoing(b):
        bx, by = lax.div(b, 2), lax.rem(b, 2)
        JA[bx, by] = times_i(A[bx, by].astype(F32)).astype(BF16)
        TX[bx, by] = (link(bx, by, bx) * edge_x(bx) * back(bx, by, 1 + bx)).astype(BF16)
        TY[by, bx] = (link(bx, by, 2 + by) * edge_y(by) * back(bx, by, 3 + by)).astype(BF16)

    each(0, 4, outgoing)
    loads[4].wait()
    jm = lane_i(256)

    def turn(t):
        rows = pl.ds(pl.multiple_of(t * 256, 256), 256)
        for c in range(2):
            HT[c, t] = H[c, rows, :].T

    each(0, 2, turn)

    each(1, NGX, lambda r: gather_in(r).wait_recv())
    MP[...] = nn(MG[...].reshape(NGX * PD, 256), jm).astype(BF16)

    def press(y, t):
        rows = pl.ds(pl.multiple_of(y * 512 + t * 256, 256), 256)
        p = nn(H[0, rows, :], MG[...].reshape(NGX * PD, 256)) + nn(H[1, rows, :], MP[...])
        return p.reshape(8, PD, 256)

    def press_other(t):
        PB[pl.ds(t * 8, 8)] = press(1 - yh, t).astype(BF16)
        swap(t).start()

    def press_own(t):
        PO[pl.ds(t * 8, 8)] = press(yh, t)

    each(0, 2, press_other)

    far_gather_in(0).wait_recv()
    opposite_gather().start()
    each(1, 5, lambda q: near_gather(q, 2).start())
    across(NZ - FAR).start()
    far_gather_in(1).wait_recv()
    each(1, 5, lambda q: near_gather(q, 1).start())
    across(FAR).start()

    each(0, 2, press_own)
    for s in range(2):
        halo_x(X, HX, 0, s).start()
        halo_y(X, HY, 1, s).start()
    for s in range(2):
        halo_x(TX, RX, 2, s).start()
        halo_y(TY, RY, 3, s).start()
    each(2, 4, turn)

    def local_forward(b):
        bx, by = lax.div(b, 2), lax.rem(b, 2)
        m = b * 5
        x = X[bx, by]
        own = nt(x, C[m, 0]) + times_i(nt(x, C[m, 1]))
        OWN[bx, by] = own
        dx, dy = 1 - bx, 3 - by
        fx, fy = link(bx, by, dx), link(bx, by, dy)
        xs, ys = X[1 - bx, by], X[bx, 1 - by]
        re = fx * nt(xs, C[m + 1 + dx, 0]) + fy * nt(ys, C[m + 1 + dy, 0])
        im = fx * nt(xs, C[m + 1 + dx, 1]) + fy * nt(ys, C[m + 1 + dy, 1])
        RES[bx, by] = own + re + times_i(im) - E[bx, by].astype(F32)

    def local_adjoint(b):
        bx, by = lax.div(b, 2), lax.rem(b, 2)
        MULT[bx, by] = (
            back(bx, by, 0)
            + link(1 - bx, by, bx) * back(1 - bx, by, 1 + bx)
            + link(bx, 1 - by, 2 + by) * back(bx, 1 - by, 3 + by))

    each(0, 4, local_adjoint)

    opposite_gather_in().wait_recv()
    across(8).start()

    def pass_on(c):
        def go(q):
            near_gather_in(q, c).wait_recv()
            across(near_slot(q, c)).start()
        each(1, 5, go)

    pass_on(0)
    pass_on(2)
    pass_on(1)

    each(0, 2, lambda t: swap(t).wait_recv())

    def add_other(t):
        PO[t] = PO[t] + YB[t].astype(F32)
        SB[t] = PO[t].astype(BF16)

    each(0, NZ, add_other)
    opposite_part().start()

    def start_parts(q):
        for c in (1, 2, 0):
            near_part(q, c).start()

    each(1, 5, start_parts)

    def turn_loads(k):
        LP[k] = nn(LG[pl.ds(k * 8, 8)].reshape(256, 256), jm).astype(BF16)

    def react(y, t):
        rows = pl.ds(pl.multiple_of(t * 256, 256), 256)
        total = jnp.zeros((256, 256), F32)
        for i in range(2):
            k = 2 * y + i
            total = total + nn(HT[0, k, rows, :], LG[pl.ds(k * 8, 8)].reshape(256, 256))
            total = total - nn(HT[1, k, rows, :], LP[k])
        return total.reshape(8, PD, 256)

    def react_own(t):
        QB[pl.ds(t * 8, 8)] = react(yh, t)

    def react_other(t):
        rows = pl.ds(t * 8, 8)
        QB[rows] = QB[rows] + react(1 - yh, t)

    each(2 * yh, 2 * yh + 2, turn_loads)
    each(0, 2, react_own)
    each(0, NZ, lambda o: across_in(o).wait_recv())
    each(2 - 2 * yh, 4 - 2 * yh, turn_loads)
    each(0, 2, react_other)
    each(1, NGX, lambda r: sum_part(r).start())

    def done_parts(q):
        for c in range(3):
            near_part(q, c).wait_recv()

    opposite_part().wait_recv()
    each(1, 5, done_parts)

    def collect(c):
        total = PO[lax.rem(z + CHUNKS[c], NZ)]
        for q in range(1, 5):
            total = total + RA[q, c].astype(F32)
        return total

    TB[0] = (collect(1) + RA[0, 0].astype(F32)).astype(BF16)
    TB[1] = collect(2).astype(BF16)
    for i in range(2):
        far_part(i).start()
    loads[5].wait()
    each(0, 4, local_forward)

    own_out = pltpu.make_async_copy(OWN, own_h, lsem.at[0])
    own_out.start()

    for s in range(2):
        halo_x(X, HX, 0, s).wait_recv()
        halo_y(X, HY, 1, s).wait_recv()

    def halo_forward(b):
        bx, by = lax.div(b, 2), lax.rem(b, 2)
        m = b * 5 + 1
        fx = link(bx, by, bx) * edge_x(bx)
        fy = link(bx, by, 2 + by) * edge_y(by)
        xs, ys = HX[bx, by], HY[by, bx]
        re = fx * nt(xs, C[m + bx, 0]) + fy * nt(ys, C[m + 2 + by, 0])
        im = fx * nt(xs, C[m + bx, 1]) + fy * nt(ys, C[m + 2 + by, 1])
        RES[bx, by] = RES[bx, by] + re + times_i(im)

    each(0, 4, halo_forward)
    res_out = pltpu.make_async_copy(RES, res_h, lsem.at[1])
    res_out.start()
    for s in range(2):
        halo_x(TX, RX, 2, s).wait_recv()
        halo_y(TY, RY, 3, s).wait_recv()

    def halo_adjoint(b):
        bx, by = lax.div(b, 2), lax.rem(b, 2)
        MULT[bx, by] = MULT[bx, by] + RX[bx, by].astype(F32) + RY[by, bx].astype(F32)

    each(0, 4, halo_adjoint)
    mult_out = pltpu.make_async_copy(MULT, mult_h, lsem.at[2])
    mult_out.start()

    for i in range(2):
        far_gather(i).wait_send()
        swap(i).wait_send()
        halo_x(X, HX, 0, i).wait_send()
        halo_y(X, HY, 1, i).wait_send()
        halo_x(TX, RX, 2, i).wait_send()
        halo_y(TY, RY, 3, i).wait_send()
    opposite_gather().wait_send()
    opposite_part().wait_send()
    each(1, NGX, lambda r: gather(r).wait_send())
    each(0, NZ, lambda o: across(o).wait_send())

    def sent_near(q):
        for c in range(3):
            near_gather(q, c).wait_send()
            near_part(q, c).wait_send()

    each(1, 5, sent_near)

    each(1, NGX, lambda r: sum_part(r).wait_recv())
    total = QB[gx]
    for r in range(1, NGX):
        total = total + RG[r]
    reaction_o[...] = total.astype(BF16)

    kept = collect(0)
    for i in range(2):
        far_part(i).wait_recv()
    pressure_o[...] = kept + RB[0].astype(F32) + RB[1].astype(F32)

    each(1, NGX, lambda r: sum_part(r).wait_send())
    for i in range(2):
        far_part(i).wait_send()
    own_out.wait()
    res_out.wait()
    mult_out.wait()


def finish(lift, scale, pressure, reaction, pmap, res_in, mult_in, own, res_o, mult_o, sens_o):
    b = pl.program_id(0)
    p = pressure[...]
    high = p.astype(BF16)
    low = (p - high.astype(F32)).astype(BF16)
    res_o[...] = res_in[...] + lift * (tn(high, pmap[...]) + tn(low, pmap[...]))
    mult = mult_in[...] + lift * tn(reaction[...], pmap[...])
    mult_o[...] = mult
    sens_o[lax.div(b, 2), lax.rem(b, 2)] = jnp.sum(mult * own[...]) * scale


def on_device(plate_motion, adjoint_load, excitation, coupling, joints, hydro, panel_map):
    lift = math.sqrt(4 * 128 / PD)
    any_ = pl.BlockSpec(memory_space=pl.ANY)
    vm = pl.BlockSpec(memory_space=pltpu.VMEM)
    sm = pl.BlockSpec(memory_space=pltpu.SMEM)
    block = (2, 2, 256, 128)
    panel = (PD, 256)
    dma = pltpu.SemaphoreType.DMA
    whole = jax.ShapeDtypeStruct(block, F32)
    res, mult, own, pressure, reaction, pmap = pl.pallas_call(
        kernel,
        out_shape=(
            whole, whole, whole,
            jax.ShapeDtypeStruct(panel, F32),
            jax.ShapeDtypeStruct(panel, BF16),
            jax.ShapeDtypeStruct((PD, 512), BF16),
        ),
        in_specs=[sm, any_, any_, any_, any_, any_, any_],
        out_specs=(any_, any_, any_, vm, vm, vm),
        scratch_shapes=[
            pltpu.VMEM(block, BF16),
            pltpu.VMEM(block, BF16),
            pltpu.VMEM(block, BF16),
            pltpu.VMEM(block, BF16),
            pltpu.VMEM((20, 2, 128, 128), BF16),
            pltpu.VMEM((2, 1024, 512), BF16),
            pltpu.VMEM((2, 4, 512, 256), BF16),
            pltpu.VMEM((128, 128), BF16),
            pltpu.VMEM((128, 128), F32),
            pltpu.VMEM((NGX,) + panel, BF16),
            pltpu.VMEM((NGX * PD, 256), BF16),
            pltpu.VMEM((NGY,) + panel, BF16),
            pltpu.VMEM((4, 256, 256), BF16),
            pltpu.VMEM((NZ,) + panel, F32),
            pltpu.VMEM((NZ,) + panel, BF16),
            pltpu.VMEM((NZ,) + panel, BF16),
            pltpu.VMEM((NZ,) + panel, BF16),
            pltpu.VMEM((5, 3) + panel, BF16),
            pltpu.VMEM((2,) + panel, BF16),
            pltpu.VMEM((2,) + panel, BF16),
            pltpu.VMEM((NGX,) + panel, F32),
            pltpu.VMEM((NGX,) + panel, F32),
            pltpu.VMEM(block, BF16),
            pltpu.VMEM(block, BF16),
            pltpu.VMEM(block, BF16),
            pltpu.VMEM(block, BF16),
            pltpu.VMEM(block, BF16),
            pltpu.VMEM(block, BF16),
            pltpu.VMEM(block, F32),
            pltpu.VMEM(block, F32),
            pltpu.VMEM(block, F32),
            dma((6,)),
            dma((NGX,)), dma((NGX,)),
            dma((2,)), dma((2,)),
            dma((5, 3)), dma((5, 3)),
            dma((NZ,)), dma((NZ,)),
            dma((2,)), dma((2,)),
            dma((5, 3)), dma((5, 3)),
            dma((2,)), dma((2,)),
            dma((NGX,)), dma((NGX,)),
            dma((4, 2)), dma((4, 2)),
        ],
        compiler_params=pltpu.CompilerParams(
            collective_id=0, has_side_effects=True, vmem_limit_bytes=62 << 20),
        name="plate",
    )(
        joints,
        plate_motion.reshape(block),
        adjoint_load.reshape(block),
        excitation.reshape(block),
        coupling.reshape(20, 2, 128, 128),
        hydro,
        panel_map.reshape(128, 128),
    )
    tile = pl.BlockSpec((None, None, 256, 128), lambda b: (b // 2, b % 2, 0, 0))
    fixed = pl.BlockSpec(panel, lambda b: (0, 0))
    res, mult, sens = pl.pallas_call(
        functools.partial(finish, lift, 1.0 / 128.0),
        grid=(4,),
        out_shape=(whole, whole, jax.ShapeDtypeStruct((2, 2), F32)),
        in_specs=[fixed, fixed, pl.BlockSpec((PD, 128), lambda b: (0, b)), tile, tile, tile],
        out_specs=(tile, tile, sm),
        compiler_params=pltpu.CompilerParams(vmem_limit_bytes=62 << 20),
        name="finish",
    )(pressure, reaction, pmap, res, mult, own)
    shape = plate_motion.shape
    return res.reshape(shape), mult.reshape(shape), sens


def solution(mesh):
    placed = (
        P("gx", "gy", None, None, None),
        P("gx", "gy", None, None, None),
        P("gx", "gy", None, None, None),
        P("gx", "gy", None, None, None, None),
        P("gx", "gy", None),
        P(None, "gx", "gy"),
        P(("gx", "gy"), None, None, None),
    )
    return jax.shard_map(
        on_device,
        mesh=mesh,
        in_specs=placed,
        out_specs=(P("gx", "gy", None, None, None), P("gx", "gy", None, None, None), P("gx", "gy")),
        check_vma=False,
    )
```

time: 441 us -> 62.1 us (0.14)
  the two profiles are of different devices: /device:TPU:14 before, /device:TPU:1 now
where the time goes in v1:
time: 62.1 us; the launch traced here: 61.9 us
  Pallas kernels  61.3 us (99%)
  between operations  0.64 us (1%)
    pallas_call x1, Pallas kernels, on_device(): pl.pallas_call(kernel, out_shape=(whole, whole, whole, jax.ShapeDtypeStru...  57.2 us
    pallas_call x1, Pallas kernels, on_device(): pl.pallas_call(functools.partial(finish, lift, 1.0 / 128.0), grid=(4,), o...  4.07 us

profile of v1, /device:TPU:1, one launch (start us, length us, event | category | flops | bytes accessed | tf_op | source)
XLA Modules:
  0.0 61.9 jit_solution(8960335597771718298)
XLA Ops:
  0.6 57.2 %plate.1 = (f32[2,2,256,128]{3,2,1,0:T(8,128)}, f32[2,2,256,128]{3,2,1,0:T(8,128)}, f32[2,2,256,128]{3,2,1,0:T(8,128)}, f32[32,256]{1,0:T(8,128)}, bf16[32,256]{1,0:T(8,128)(2,1)}, /*index=5*/bf16[32,512]{1,0:T(8,128)(2,1)}) custom-call(s32[2,2,4]{2,1,0:T(2,128)} %joints.1, bf16[2,2,256,128]{3,2,1,0:T(8,128)(2,1)} %bitcast.8, ...), custom_call_target="tpu_custom_call" | custom-call | tf_op jit(solution)/shard_map/plate/pallas_call | solution.py:450
  57.9 4.1 %finish.1 = (f32[2,2,256,128]{3,2,1,0:T(8,128)}, f32[2,2,256,128]{3,2,1,0:T(8,128)}, f32[2,2]{1,0:T(2,128)}) custom-call(f32[32,256]{1,0:T(8,128)} %get-tuple-element.12.pressure, bf16[32,256]{1,0:T(8,128)(2,1)} %get-tuple-element.13.reaction, bf16[32,512]{1,0:T(8,128)(2,1)} %get-tuple-element.14.pmap, f32[2,2,256,128]{3,2,1,0:T(8,128)} %get-tuple-element.15.res_in, ...), custom_call_target="tpu_custom_call" | custom-call | tf_op jit(solution)/shard_map/finish/pallas_call | solution.py:517

commit v2 on v1

--- a/solution.py
+++ b/solution.py
@@ -45,11 +45,11 @@
 
 
 def kernel(
-    joints, plate_h, adj_h, exc_h, coup_h, hyd_h, pmap_h,
-    res_h, mult_h, own_h, pressure_o, reaction_o, map_o,
-    X, A, JA, E, C, H, HT, PM, PM32, MG, MP, LG, LP, PO, PB, YB, SB, RA, TB, RB, QB, RG,
-    HX, HY, TX, TY, RX, RY, RES, MULT, OWN,
-    lsem, gx_s, gx_r, fa_s, fa_r, nb_s, nb_r, yf_s, yf_r, yx_s, yx_r,
+    joints_h, plate_h, adj_h, exc_h, coup_h, hyd_h, pmap_h,
+    RES, MULT, OWN, pressure_o, reaction_o, map_o,
+    X, A, JA, E, C, H, HT, PM, PM32, MG, MP, LG, LP, PB, RA, T, TB, RB, QB, RG,
+    HX, HY, TX, TY, RX, RY, joints,
+    lsem, gx_s, gx_r, fa_s, fa_r, nb_s, nb_r, yf_s, yf_r,
     ra_s, ra_r, rb_s, rb_r, rx_s, rx_r, h_s, h_r,
 ):
     gx = lax.axis_index("gx")
@@ -79,7 +79,8 @@
     loads = [
         pltpu.make_async_copy(s, d, lsem.at[i])
         for i, (s, d) in enumerate(
-            ((pmap_h, PM), (adj_h, A), (plate_h, X), (coup_h, C), (hyd_h, H), (exc_h, E))
+            ((pmap_h, PM), (adj_h, A), (plate_h, X), (coup_h, C), (hyd_h, H), (exc_h, E),
+             (joints_h, joints))
         )
     ]
     for c in loads:
@@ -141,33 +142,38 @@
         slot = gy_at(o, 1)
         return remote(LG.at[slot], LG.at[slot], yf_s.at[o], yf_r.at[o], (gx, gy_at(0, 1)))
 
-    def swap(t):
-        rows = pl.ds(t * 8, 8)
-        return remote(PB.at[rows], YB.at[rows], yx_s.at[t], yx_r.at[t], (gx, gy_at(0, 1)))
-
     def near_part(q, c):
-        return remote(SB.at[lax.rem(z + near(q) + CHUNKS[c], NZ)], RA.at[q, c],
+        return remote(PB.at[:, lax.rem(z + near(q) + CHUNKS[c], NZ)], RA.at[q, c],
                       ra_s.at[q, c], ra_r.at[q, c], (gx, gy_at(near(q), 0)))
 
     def opposite_part():
-        return remote(SB.at[lax.rem(z + 8, NZ)], RA.at[0, 0],
+        return remote(PB.at[:, lax.rem(z + 8, NZ)], RA.at[0, 0],
                       ra_s.at[0, 0], ra_r.at[0, 0], (gx, gy_at(3, 0)))
 
     def far_part(i):
-        return remote(TB.at[i], RB.at[i], rb_s.at[i], rb_r.at[i],
-                      (gx, gy_at((FAR, NZ - FAR)[i], 0)))
+        dz, dy = ((0, 1), (FAR, 0), (NZ - FAR, 0), (FAR, 1), (NZ - FAR, 1))[i]
+        return remote(TB.at[i], RB.at[i], rb_s.at[i], rb_r.at[i], (gx, gy_at(dz, dy)))
 
     def sum_part(r):
         return remote(QB.at[gx_at(r)], RG.at[r], rx_s.at[r], rx_r.at[r], (gx_at(r), gy))
 
+    def side(gap, s):
+        return gap if s else -gap
+
     def halo_x(src, dst, k, s):
         return remote(src.at[s], dst.at[1 - s], h_s.at[k, s], h_r.at[k, 1 - s],
-                      (gx_at(1 if s else NGX - 1), gy))
+                      (gx + side(1, s), gy))
+
+    def halo_x_in(src, dst, k, s):
+        return remote(src.at[s], dst.at[s], h_s.at[k, s], h_r.at[k, s], (gx + side(1, s), gy))
 
     def halo_y(src, dst, k, s):
         return remote(src.at[:, s] if k == 1 else src.at[s], dst.at[1 - s],
-                      h_s.at[k, s], h_r.at[k, 1 - s],
-                      (gx, lax.rem(gy + (1 if s else NGY - 1), NGY)))
+                      h_s.at[k, s], h_r.at[k, 1 - s], (gx, gy + side(1, s)))
+
+    def halo_y_in(src, dst, k, s):
+        return remote(src.at[:, s] if k == 1 else src.at[s], dst.at[s],
+                      h_s.at[k, s], h_r.at[k, s], (gx, gy + side(1, s)))
 
     loads[0].wait()
     PM32[...] = PM[...].astype(F32)
@@ -185,15 +191,8 @@
     loads[2].wait()
     MG[gx] = panels(X)
 
-    pl.semaphore_wait(bar, 4 + 1 + 2 + 4 + 15)
-
-    for i in range(2):
-        far_gather(i).start()
-    each(1, NGX, lambda r: gather(r).start())
-    across(0).start()
-    each(1, 5, lambda q: near_gather(q, 0).start())
-
     loads[3].wait()
+    loads[6].wait()
 
     def link(bx, by, d):
         return joints[bx, by, d].astype(F32)
@@ -217,6 +216,65 @@
         TY[by, bx] = (link(bx, by, 2 + by) * edge_y(by) * back(bx, by, 3 + by)).astype(BF16)
 
     each(0, 4, outgoing)
+    def to_x(s):
+        return gx + 1 < NGX if s else gx > 0
+
+    def to_y(s):
+        return gy + 1 < NGY if s else gy > 0
+
+    def sent_halos(s):
+        @pl.when(to_x(s))
+        def _():
+            halo_x(X, HX, 0, s).wait_send()
+            halo_x(TX, RX, 2, s).wait_send()
+
+        @pl.when(to_y(s))
+        def _():
+            halo_y(X, HY, 1, s).wait_send()
+            halo_y(TY, RY, 3, s).wait_send()
+
+    def crosses(s):
+        return z == NZ - 1 if s else z == 0
+
+    def start_crossing():
+        for s in range(2):
+            @pl.when(jnp.logical_and(to_y(s), crosses(s)))
+            def _():
+                halo_y(X, HY, 1, s).start()
+                halo_y(TY, RY, 3, s).start()
+
+    def start_halos(k):
+        for s in range(2):
+            @pl.when(to_x(s))
+            def _():
+                halo_x(*((X, HX), (TX, RX))[k], 2 * k, s).start()
+
+            @pl.when(jnp.logical_and(to_y(s), jnp.logical_not(crosses(s))))
+            def _():
+                halo_y(*((X, HY), (TY, RY))[k], 2 * k + 1, s).start()
+
+    def wait_halos(k):
+        for s in range(2):
+            @pl.when(to_x(s))
+            def _():
+                src, dst = ((X, HX), (TX, RX))[k]
+                halo_x_in(src, dst, 2 * k, s).wait_recv()
+
+            @pl.when(to_y(s))
+            def _():
+                src, dst = ((X, HY), (TY, RY))[k]
+                halo_y_in(src, dst, 2 * k + 1, s).wait_recv()
+
+    pl.semaphore_wait(bar, 4 + 1 + 2 + 4 + 15)
+
+    for i in range(2):
+        far_gather(i).start()
+    each(1, NGX, lambda r: gather(r).start())
+    across(0).start()
+    start_crossing()
+    start_halos(0)
+    each(1, 5, lambda q: near_gather(q, 0).start())
+
     loads[4].wait()
     jm = lane_i(256)
 
@@ -227,38 +285,38 @@
 
     each(0, 2, turn)
 
-    each(1, NGX, lambda r: gather_in(r).wait_recv())
-    MP[...] = nn(MG[...].reshape(NGX * PD, 256), jm).astype(BF16)
-
-    def press(y, t):
-        rows = pl.ds(pl.multiple_of(y * 512 + t * 256, 256), 256)
-        p = nn(H[0, rows, :], MG[...].reshape(NGX * PD, 256)) + nn(H[1, rows, :], MP[...])
-        return p.reshape(8, PD, 256)
-
-    def press_other(t):
-        PB[pl.ds(t * 8, 8)] = press(1 - yh, t).astype(BF16)
-        swap(t).start()
-
-    def press_own(t):
-        PO[pl.ds(t * 8, 8)] = press(yh, t)
-
-    each(0, 2, press_other)
+    def pass_on(c):
+        def go(q):
+            near_gather_in(q, c).wait_recv()
+            across(near_slot(q, c)).start()
+        each(1, 5, go)
 
     far_gather_in(0).wait_recv()
     opposite_gather().start()
     each(1, 5, lambda q: near_gather(q, 2).start())
-    across(NZ - FAR).start()
     far_gather_in(1).wait_recv()
     each(1, 5, lambda q: near_gather(q, 1).start())
+
+    each(1, NGX, lambda r: gather_in(r).wait_recv())
+    MP[...] = nn(MG[...].reshape(NGX * PD, 256), jm).astype(BF16)
+
+    def press(t):
+        rows = pl.ds(pl.multiple_of(t * 256, 256), 256)
+        p = nn(H[0, rows, :], MG[...].reshape(NGX * PD, 256)) + nn(H[1, rows, :], MP[...])
+        PB[lax.div(t, 2), pl.ds(lax.rem(t, 2) * 8, 8)] = p.astype(BF16).reshape(8, PD, 256)
+
+    each(0, 4, press)
+
+    def start_parts(q):
+        for c in (1, 2, 0):
+            near_part(q, c).start()
+
+    opposite_part().start()
+    each(1, 5, start_parts)
+    across(NZ - FAR).start()
     across(FAR).start()
-
-    each(0, 2, press_own)
-    for s in range(2):
-        halo_x(X, HX, 0, s).start()
-        halo_y(X, HY, 1, s).start()
-    for s in range(2):
-        halo_x(TX, RX, 2, s).start()
-        halo_y(TY, RY, 3, s).start()
+    pass_on(0)
+
     each(2, 4, turn)
 
     def local_forward(b):
@@ -286,30 +344,9 @@
     opposite_gather_in().wait_recv()
     across(8).start()
 
-    def pass_on(c):
-        def go(q):
-            near_gather_in(q, c).wait_recv()
-            across(near_slot(q, c)).start()
-        each(1, 5, go)
-
-    pass_on(0)
     pass_on(2)
     pass_on(1)
-
-    each(0, 2, lambda t: swap(t).wait_recv())
-
-    def add_other(t):
-        PO[t] = PO[t] + YB[t].astype(F32)
-        SB[t] = PO[t].astype(BF16)
-
-    each(0, NZ, add_other)
-    opposite_part().start()
-
-    def start_parts(q):
-        for c in (1, 2, 0):
-            near_part(q, c).start()
-
-    each(1, 5, start_parts)
+    start_halos(1)
 
     def turn_loads(k):
         LP[k] = nn(LG[pl.ds(k * 8, 8)].reshape(256, 256), jm).astype(BF16)
@@ -344,58 +381,45 @@
     opposite_part().wait_recv()
     each(1, 5, done_parts)
 
-    def collect(c):
-        total = PO[lax.rem(z + CHUNKS[c], NZ)]
-        for q in range(1, 5):
-            total = total + RA[q, c].astype(F32)
-        return total
-
-    TB[0] = (collect(1) + RA[0, 0].astype(F32)).astype(BF16)
-    TB[1] = collect(2).astype(BF16)
-    for i in range(2):
+    for c in range(3):
+        total = PB[:, lax.rem(z + CHUNKS[c], NZ)].astype(F32)
+        for q in range(0 if c == 1 else 1, 5):
+            total = total + RA[q, c if q else 0].astype(F32)
+        T[c] = total
+    for i, (c, dy) in enumerate(((0, 1), (1, 0), (2, 0), (1, 1), (2, 1))):
+        TB[i] = T[c, lax.rem(yh + dy, 2)].astype(BF16)
+    for i in (4, 3, 2, 1, 0):
         far_part(i).start()
     loads[5].wait()
     each(0, 4, local_forward)
 
-    own_out = pltpu.make_async_copy(OWN, own_h, lsem.at[0])
-    own_out.start()
-
-    for s in range(2):
-        halo_x(X, HX, 0, s).wait_recv()
-        halo_y(X, HY, 1, s).wait_recv()
+    wait_halos(0)
 
     def halo_forward(b):
         bx, by = lax.div(b, 2), lax.rem(b, 2)
         m = b * 5 + 1
         fx = link(bx, by, bx) * edge_x(bx)
         fy = link(bx, by, 2 + by) * edge_y(by)
-        xs, ys = HX[bx, by], HY[by, bx]
+        xs = jnp.where(edge_x(bx) > 0.5, HX[bx, by], jnp.zeros((256, 128), BF16))
+        ys = jnp.where(edge_y(by) > 0.5, HY[by, bx], jnp.zeros((256, 128), BF16))
         re = fx * nt(xs, C[m + bx, 0]) + fy * nt(ys, C[m + 2 + by, 0])
         im = fx * nt(xs, C[m + bx, 1]) + fy * nt(ys, C[m + 2 + by, 1])
         RES[bx, by] = RES[bx, by] + re + times_i(im)
 
     each(0, 4, halo_forward)
-    res_out = pltpu.make_async_copy(RES, res_h, lsem.at[1])
-    res_out.start()
-    for s in range(2):
-        halo_x(TX, RX, 2, s).wait_recv()
-        halo_y(TY, RY, 3, s).wait_recv()
+    wait_halos(1)
 
     def halo_adjoint(b):
         bx, by = lax.div(b, 2), lax.rem(b, 2)
-        MULT[bx, by] = MULT[bx, by] + RX[bx, by].astype(F32) + RY[by, bx].astype(F32)
+        xs = jnp.where(edge_x(bx) > 0.5, RX[bx, by].astype(F32), 0.0)
+        ys = jnp.where(edge_y(by) > 0.5, RY[by, bx].astype(F32), 0.0)
+        MULT[bx, by] = MULT[bx, by] + xs + ys
 
     each(0, 4, halo_adjoint)
-    mult_out = pltpu.make_async_copy(MULT, mult_h, lsem.at[2])
-    mult_out.start()
 
     for i in range(2):
         far_gather(i).wait_send()
-        swap(i).wait_send()
-        halo_x(X, HX, 0, i).wait_send()
-        halo_y(X, HY, 1, i).wait_send()
-        halo_x(TX, RX, 2, i).wait_send()
-        halo_y(TY, RY, 3, i).wait_send()
+        sent_halos(i)
     opposite_gather().wait_send()
     opposite_part().wait_send()
     each(1, NGX, lambda r: gather(r).wait_send())
@@ -414,33 +438,41 @@
         total = total + RG[r]
     reaction_o[...] = total.astype(BF16)
 
-    kept = collect(0)
-    for i in range(2):
+    total = T[0, yh]
+    for i in range(5):
         far_part(i).wait_recv()
-    pressure_o[...] = kept + RB[0].astype(F32) + RB[1].astype(F32)
+        total = total + RB[i].astype(F32)
+    pressure_o[...] = total
 
     each(1, NGX, lambda r: sum_part(r).wait_send())
-    for i in range(2):
+    for i in range(5):
         far_part(i).wait_send()
-    own_out.wait()
-    res_out.wait()
-    mult_out.wait()
-
-
-def finish(lift, scale, pressure, reaction, pmap, res_in, mult_in, own, res_o, mult_o, sens_o):
-    b = pl.program_id(0)
+
+
+def finish(lift, scale, pressure, reaction, pmap, res_in, mult_in, own, res_h, mult_h, sens_o,
+           res_v, mult_v, sem):
     p = pressure[...]
     high = p.astype(BF16)
     low = (p - high.astype(F32)).astype(BF16)
-    res_o[...] = res_in[...] + lift * (tn(high, pmap[...]) + tn(low, pmap[...]))
-    mult = mult_in[...] + lift * tn(reaction[...], pmap[...])
-    mult_o[...] = mult
-    sens_o[lax.div(b, 2), lax.rem(b, 2)] = jnp.sum(mult * own[...]) * scale
+    copies = []
+    for b in range(4):
+        at = (b // 2, b % 2)
+        m = pmap[:, b * 128:(b + 1) * 128]
+        mult = mult_in[at] + lift * tn(reaction[...], m)
+        mult_v[at] = mult
+        copies.append(pltpu.make_async_copy(mult_v.at[at], mult_h.at[at], sem.at[0, b]))
+        copies[-1].start()
+        res_v[at] = res_in[at] + lift * (tn(high, m) + tn(low, m))
+        copies.append(pltpu.make_async_copy(res_v.at[at], res_h.at[at], sem.at[1, b]))
+        copies[-1].start()
+        sens_o[at] = jnp.sum(mult * own[at]) * scale
+    for c in copies:
+        c.wait()
 
 
 def on_device(plate_motion, adjoint_load, excitation, coupling, joints, hydro, panel_map):
     lift = math.sqrt(4 * 128 / PD)
-    any_ = pl.BlockSpec(memory_space=pl.ANY)
+    hbm = pl.BlockSpec(memory_space=pltpu.HBM)
     vm = pl.BlockSpec(memory_space=pltpu.VMEM)
     sm = pl.BlockSpec(memory_space=pltpu.SMEM)
     block = (2, 2, 256, 128)
@@ -455,8 +487,8 @@
             jax.ShapeDtypeStruct(panel, BF16),
             jax.ShapeDtypeStruct((PD, 512), BF16),
         ),
-        in_specs=[sm, any_, any_, any_, any_, any_, any_],
-        out_specs=(any_, any_, any_, vm, vm, vm),
+        in_specs=[hbm] * 7,
+        out_specs=(vm,) * 6,
         scratch_shapes=[
             pltpu.VMEM(block, BF16),
             pltpu.VMEM(block, BF16),
@@ -471,13 +503,11 @@
             pltpu.VMEM((NGX * PD, 256), BF16),
             pltpu.VMEM((NGY,) + panel, BF16),
             pltpu.VMEM((4, 256, 256), BF16),
-            pltpu.VMEM((NZ,) + panel, F32),
-            pltpu.VMEM((NZ,) + panel, BF16),
-            pltpu.VMEM((NZ,) + panel, BF16),
-            pltpu.VMEM((NZ,) + panel, BF16),
-            pltpu.VMEM((5, 3) + panel, BF16),
-            pltpu.VMEM((2,) + panel, BF16),
-            pltpu.VMEM((2,) + panel, BF16),
+            pltpu.VMEM((2, NZ) + panel, BF16),
+            pltpu.VMEM((5, 3, 2) + panel, BF16),
+            pltpu.VMEM((3, 2) + panel, F32),
+            pltpu.VMEM((5,) + panel, BF16),
+            pltpu.VMEM((5,) + panel, BF16),
             pltpu.VMEM((NGX,) + panel, F32),
             pltpu.VMEM((NGX,) + panel, F32),
             pltpu.VMEM(block, BF16),
@@ -486,41 +516,37 @@
             pltpu.VMEM(block, BF16),
             pltpu.VMEM(block, BF16),
             pltpu.VMEM(block, BF16),
-            pltpu.VMEM(block, F32),
-            pltpu.VMEM(block, F32),
-            pltpu.VMEM(block, F32),
-            dma((6,)),
+            pltpu.SMEM((2, 2, 4), jnp.int32),
+            dma((7,)),
             dma((NGX,)), dma((NGX,)),
             dma((2,)), dma((2,)),
             dma((5, 3)), dma((5, 3)),
             dma((NZ,)), dma((NZ,)),
-            dma((2,)), dma((2,)),
             dma((5, 3)), dma((5, 3)),
-            dma((2,)), dma((2,)),
+            dma((5,)), dma((5,)),
             dma((NGX,)), dma((NGX,)),
             dma((4, 2)), dma((4, 2)),
         ],
         compiler_params=pltpu.CompilerParams(
-            collective_id=0, has_side_effects=True, vmem_limit_bytes=62 << 20),
+            collective_id=0, has_side_effects=True, vmem_limit_bytes=32 << 20),
         name="plate",
     )(
-        joints,
-        plate_motion.reshape(block),
-        adjoint_load.reshape(block),
-        excitation.reshape(block),
-        coupling.reshape(20, 2, 128, 128),
-        hydro,
-        panel_map.reshape(128, 128),
+        *(pltpu.with_memory_space_constraint(x, pltpu.HBM) for x in (
+            joints,
+            plate_motion.reshape(block),
+            adjoint_load.reshape(block),
+            excitation.reshape(block),
+            coupling.reshape(20, 2, 128, 128),
+            hydro,
+            panel_map.reshape(128, 128))),
     )
-    tile = pl.BlockSpec((None, None, 256, 128), lambda b: (b // 2, b % 2, 0, 0))
-    fixed = pl.BlockSpec(panel, lambda b: (0, 0))
     res, mult, sens = pl.pallas_call(
         functools.partial(finish, lift, 1.0 / 128.0),
-        grid=(4,),
         out_shape=(whole, whole, jax.ShapeDtypeStruct((2, 2), F32)),
-        in_specs=[fixed, fixed, pl.BlockSpec((PD, 128), lambda b: (0, b)), tile, tile, tile],
-        out_specs=(tile, tile, sm),
-        compiler_params=pltpu.CompilerParams(vmem_limit_bytes=62 << 20),
+        in_specs=[vm] * 6,
+        out_specs=(hbm, hbm, sm),
+        scratch_shapes=[pltpu.VMEM(block, F32)] * 2 + [dma((2, 4))],
+        compiler_params=pltpu.CompilerParams(vmem_limit_bytes=32 << 20),
         name="finish",
     )(pressure, reaction, pmap, res, mult, own)
     shape = plate_motion.shape

time: 62.1 us -> 53.8 us (0.87)
  the two profiles are of different devices: /device:TPU:1 before, /device:TPU:17 now
where the time goes in v2:
time: 53.8 us; the launch traced here: 53.6 us
  Pallas kernels  53 us (99%)
  between operations  0.64 us (1%)
    pallas_call x1, Pallas kernels, on_device(): pl.pallas_call(kernel, out_shape=(whole, whole, whole, jax.ShapeDtypeStru...  51.1 us
    pallas_call x1, Pallas kernels, on_device(): pl.pallas_call(functools.partial(finish, lift, 1.0 / 128.0), out_shape=(w...  1.86 us

profile of v2, /device:TPU:17, one launch (start us, length us, event | category | flops | bytes accessed | tf_op | source)
XLA Modules:
  0.0 53.6 jit_solution(939004478820197588)
XLA Ops:
  0.6 51.1 %plate.1 = (f32[2,2,256,128]{3,2,1,0:T(8,128)S(1)}, f32[2,2,256,128]{3,2,1,0:T(8,128)S(1)}, f32[2,2,256,128]{3,2,1,0:T(8,128)S(1)}, f32[32,256]{1,0:T(8,128)S(1)...) custom-call(s32[2,2,4]{2,1,0:T(2,128)} %joints_h.1, bf16[2,2,256,128]{3,2,1,0:T(8,128)(2,1)} %bitcast.8, ...), custom_call_target="tpu_custom_call" | custom-call | tf_op jit(solution)/shard_map/plate/pallas_call | solution.py:482
  51.8 1.9 %finish.1 = (f32[2,2,256,128]{3,2,1,0:T(8,128)}, f32[2,2,256,128]{3,2,1,0:T(8,128)}, f32[2,2]{1,0:T(2,128)}) custom-call(f32[32,256]{1,0:T(8,128)S(1)} %get-tuple-element.12.pressure, bf16[32,256]{1,0:T(8,128)(2,1)S(1)} %get-tuple-element.13.reaction, bf16[32,512]{1,0:T(8,128)(2,1)S(1)} %get-tuple-element.14.pmap, ...), custom_call_target="tpu_custom_call" | custom-call | tf_op jit(solution)/shard_map/finish/pallas_call | solution.py:543

commit v3 on v2

--- a/solution.py
+++ b/solution.py
@@ -271,7 +271,6 @@
         far_gather(i).start()
     each(1, NGX, lambda r: gather(r).start())
     across(0).start()
-    start_crossing()
     start_halos(0)
     each(1, 5, lambda q: near_gather(q, 0).start())
 
@@ -313,6 +312,7 @@
 
     opposite_part().start()
     each(1, 5, start_parts)
+    start_crossing()
     across(NZ - FAR).start()
     across(FAR).start()
     pass_on(0)
@@ -339,7 +339,6 @@
             + link(1 - bx, by, bx) * back(1 - bx, by, 1 + bx)
             + link(bx, 1 - by, 2 + by) * back(bx, 1 - by, 3 + by))
 
-    each(0, 4, local_adjoint)
 
     opposite_gather_in().wait_recv()
     across(8).start()
@@ -392,6 +391,7 @@
         far_part(i).start()
     loads[5].wait()
     each(0, 4, local_forward)
+    each(0, 4, local_adjoint)
 
     wait_halos(0)
 

time: 53.8 us -> 50.4 us (0.937)
  the two profiles are of different devices: /device:TPU:17 before, /device:TPU:1 now
where the time goes in v3:
time: 50.4 us; the launch traced here: 50.3 us
  Pallas kernels  49.6 us (98%)
  between operations  0.64 us (1%)
    pallas_call x1, Pallas kernels, on_device(): pl.pallas_call(kernel, out_shape=(whole, whole, whole, jax.ShapeDtypeStru...  47.8 us
    pallas_call x1, Pallas kernels, on_device(): pl.pallas_call(functools.partial(finish, lift, 1.0 / 128.0), out_shape=(w...  1.87 us

profile of v3, /device:TPU:1, one launch (start us, length us, event | category | flops | bytes accessed | tf_op | source)
XLA Modules:
  0.0 50.3 jit_solution(1149266812889495396)
XLA Ops:
  0.6 47.8 %plate.1 = (f32[2,2,256,128]{3,2,1,0:T(8,128)S(1)}, f32[2,2,256,128]{3,2,1,0:T(8,128)S(1)}, f32[2,2,256,128]{3,2,1,0:T(8,128)S(1)}, f32[32,256]{1,0:T(8,128)S(1)...) custom-call(s32[2,2,4]{2,1,0:T(2,128)} %joints_h.1, bf16[2,2,256,128]{3,2,1,0:T(8,128)(2,1)} %bitcast.8, ...), custom_call_target="tpu_custom_call" | custom-call | tf_op jit(solution)/shard_map/plate/pallas_call | solution.py:482
  48.4 1.9 %finish.1 = (f32[2,2,256,128]{3,2,1,0:T(8,128)}, f32[2,2,256,128]{3,2,1,0:T(8,128)}, f32[2,2]{1,0:T(2,128)}) custom-call(f32[32,256]{1,0:T(8,128)S(1)} %get-tuple-element.12.pressure, bf16[32,256]{1,0:T(8,128)(2,1)S(1)} %get-tuple-element.13.reaction, bf16[32,512]{1,0:T(8,128)(2,1)S(1)} %get-tuple-element.14.pmap, ...), custom_call_target="tpu_custom_call" | custom-call | tf_op jit(solution)/shard_map/finish/pallas_call | solution.py:543

commit v4 on v3

--- a/solution.py
+++ b/solution.py
@@ -47,10 +47,10 @@
 def kernel(
     joints_h, plate_h, adj_h, exc_h, coup_h, hyd_h, pmap_h,
     RES, MULT, OWN, pressure_o, reaction_o, map_o,
-    X, A, JA, E, C, H, HT, PM, PM32, MG, MP, LG, LP, PB, RA, T, TB, RB, QB, RG,
+    X, A, JA, E, C, H, HT, PM, PM32, MG, MP, LG, LP, PB, RA, T, TB, RB, QB, QC, QS, RG,
     HX, HY, TX, TY, RX, RY, joints,
     lsem, gx_s, gx_r, fa_s, fa_r, nb_s, nb_r, yf_s, yf_r,
-    ra_s, ra_r, rb_s, rb_r, rx_s, rx_r, h_s, h_r,
+    ra_s, ra_r, rb_s, rb_r, rc_s, rc_r, rx_s, rx_r, h_s, h_r,
 ):
     gx = lax.axis_index("gx")
     gy = lax.axis_index("gy")
@@ -154,8 +154,20 @@
         dz, dy = ((0, 1), (FAR, 0), (NZ - FAR, 0), (FAR, 1), (NZ - FAR, 1))[i]
         return remote(TB.at[i], RB.at[i], rb_s.at[i], rb_r.at[i], (gx, gy_at(dz, dy)))
 
+    core = lax.rem(gx, 2)
+    chip = lax.div(gx, 2)
+
+    def chip_at(r):
+        return lax.rem(chip + r, NGX // 2)
+
+    def core_part(t):
+        rows = pl.ds(t * 4, 4)
+        return remote(QB.at[rows, 1 - core], QC.at[rows], rc_s.at[t], rc_r.at[t],
+                      (gx + 1 - 2 * core, gy))
+
     def sum_part(r):
-        return remote(QB.at[gx_at(r)], RG.at[r], rx_s.at[r], rx_r.at[r], (gx_at(r), gy))
+        return remote(QS.at[chip_at(r)], RG.at[r], rx_s.at[r], rx_r.at[r],
+                      (2 * chip_at(r) + core, gy))
 
     def side(gap, s):
         return gap if s else -gap
@@ -236,12 +248,11 @@
     def crosses(s):
         return z == NZ - 1 if s else z == 0
 
-    def start_crossing():
+    def start_crossing(k):
         for s in range(2):
             @pl.when(jnp.logical_and(to_y(s), crosses(s)))
             def _():
-                halo_y(X, HY, 1, s).start()
-                halo_y(TY, RY, 3, s).start()
+                halo_y(*((X, HY), (TY, RY))[k], 2 * k + 1, s).start()
 
     def start_halos(k):
         for s in range(2):
@@ -312,7 +323,6 @@
 
     opposite_part().start()
     each(1, 5, start_parts)
-    start_crossing()
     across(NZ - FAR).start()
     across(FAR).start()
     pass_on(0)
@@ -345,6 +355,8 @@
 
     pass_on(2)
     pass_on(1)
+    start_crossing(0)
+    start_crossing(1)
     start_halos(1)
 
     def turn_loads(k):
@@ -357,21 +369,21 @@
             k = 2 * y + i
             total = total + nn(HT[0, k, rows, :], LG[pl.ds(k * 8, 8)].reshape(256, 256))
             total = total - nn(HT[1, k, rows, :], LP[k])
-        return total.reshape(8, PD, 256)
+        return total.reshape(4, 2, PD, 256)
 
     def react_own(t):
-        QB[pl.ds(t * 8, 8)] = react(yh, t)
+        QB[pl.ds(t * 4, 4)] = react(yh, t)
 
     def react_other(t):
-        rows = pl.ds(t * 8, 8)
+        rows = pl.ds(t * 4, 4)
         QB[rows] = QB[rows] + react(1 - yh, t)
+        core_part(t).start()
 
     each(2 * yh, 2 * yh + 2, turn_loads)
     each(0, 2, react_own)
     each(0, NZ, lambda o: across_in(o).wait_recv())
     each(2 - 2 * yh, 4 - 2 * yh, turn_loads)
     each(0, 2, react_other)
-    each(1, NGX, lambda r: sum_part(r).start())
 
     def done_parts(q):
         for c in range(3):
@@ -389,6 +401,11 @@
         TB[i] = T[c, lax.rem(yh + dy, 2)].astype(BF16)
     for i in (4, 3, 2, 1, 0):
         far_part(i).start()
+    for t in range(2):
+        core_part(t).wait_recv()
+    QS[...] = QB[:, core] + QC[...]
+    each(1, NGX // 2, lambda r: sum_part(r).start())
+
     loads[5].wait()
     each(0, 4, local_forward)
     each(0, 4, local_adjoint)
@@ -432,9 +449,9 @@
 
     each(1, 5, sent_near)
 
-    each(1, NGX, lambda r: sum_part(r).wait_recv())
-    total = QB[gx]
-    for r in range(1, NGX):
+    each(1, NGX // 2, lambda r: sum_part(r).wait_recv())
+    total = QS[chip]
+    for r in range(1, NGX // 2):
         total = total + RG[r]
     reaction_o[...] = total.astype(BF16)
 
@@ -444,7 +461,9 @@
         total = total + RB[i].astype(F32)
     pressure_o[...] = total
 
-    each(1, NGX, lambda r: sum_part(r).wait_send())
+    each(1, NGX // 2, lambda r: sum_part(r).wait_send())
+    for t in range(2):
+        core_part(t).wait_send()
     for i in range(5):
         far_part(i).wait_send()
 
@@ -508,8 +527,10 @@
             pltpu.VMEM((3, 2) + panel, F32),
             pltpu.VMEM((5,) + panel, BF16),
             pltpu.VMEM((5,) + panel, BF16),
-            pltpu.VMEM((NGX,) + panel, F32),
-            pltpu.VMEM((NGX,) + panel, F32),
+            pltpu.VMEM((NGX // 2, 2) + panel, F32),
+            pltpu.VMEM((NGX // 2,) + panel, F32),
+            pltpu.VMEM((NGX // 2,) + panel, F32),
+            pltpu.VMEM((NGX // 2,) + panel, F32),
             pltpu.VMEM(block, BF16),
             pltpu.VMEM(block, BF16),
             pltpu.VMEM(block, BF16),
@@ -524,7 +545,8 @@
             dma((NZ,)), dma((NZ,)),
             dma((5, 3)), dma((5, 3)),
             dma((5,)), dma((5,)),
-            dma((NGX,)), dma((NGX,)),
+            dma((2,)), dma((2,)),
+            dma((NGX // 2,)), dma((NGX // 2,)),
             dma((4, 2)), dma((4, 2)),
         ],
         compiler_params=pltpu.CompilerParams(

time: 50.4 us -> 48.3 us (0.958)
  Pallas kernels: 49.6 us -> 47.5 us
    pallas_call x1, Pallas kernels: 47.8 us -> 45.7 us  [on_device(): pl.pallas_call(kernel, out_shape=(whole, whole, whole, jax.ShapeDtypeStru...]
where the time goes in v4:
time: 48.3 us; the launch traced here: 48.2 us
  Pallas kernels  47.5 us (98%)
  between operations  0.64 us (1%)
    pallas_call x1, Pallas kernels, on_device(): pl.pallas_call(kernel, out_shape=(whole, whole, whole, jax.ShapeDtypeStru...  45.7 us
    pallas_call x1, Pallas kernels, on_device(): pl.pallas_call(functools.partial(finish, lift, 1.0 / 128.0), out_shape=(w...  1.87 us

profile of v4, /device:TPU:1, one launch (start us, length us, event | category | flops | bytes accessed | tf_op | source)
XLA Modules:
  0.0 48.2 jit_solution(969676592416847819)
XLA Ops:
  0.6 45.7 %plate.1 = (f32[2,2,256,128]{3,2,1,0:T(8,128)S(1)}, f32[2,2,256,128]{3,2,1,0:T(8,128)S(1)}, f32[2,2,256,128]{3,2,1,0:T(8,128)S(1)}, f32[32,256]{1,0:T(8,128)S(1)...) custom-call(s32[2,2,4]{2,1,0:T(2,128)} %joints_h.1, bf16[2,2,256,128]{3,2,1,0:T(8,128)(2,1)} %bitcast.8, ...), custom_call_target="tpu_custom_call" | custom-call | tf_op jit(solution)/shard_map/plate/pallas_call | solution.py:501
  46.3 1.9 %finish.1 = (f32[2,2,256,128]{3,2,1,0:T(8,128)}, f32[2,2,256,128]{3,2,1,0:T(8,128)}, f32[2,2]{1,0:T(2,128)}) custom-call(f32[32,256]{1,0:T(8,128)S(1)} %get-tuple-element.12.pressure, bf16[32,256]{1,0:T(8,128)(2,1)S(1)} %get-tuple-element.13.reaction, bf16[32,512]{1,0:T(8,128)(2,1)S(1)} %get-tuple-element.14.pmap, ...), custom_call_target="tpu_custom_call" | custom-call | tf_op jit(solution)/shard_map/finish/pallas_call | solution.py:565

commit v5 on v4

--- a/solution.py
+++ b/solution.py
@@ -203,8 +203,6 @@
     loads[2].wait()
     MG[gx] = panels(X)
 
-    loads[3].wait()
-    loads[6].wait()
 
     def link(bx, by, d):
         return joints[bx, by, d].astype(F32)
@@ -227,7 +225,6 @@
         TX[bx, by] = (link(bx, by, bx) * edge_x(bx) * back(bx, by, 1 + bx)).astype(BF16)
         TY[by, bx] = (link(bx, by, 2 + by) * edge_y(by) * back(bx, by, 3 + by)).astype(BF16)
 
-    each(0, 4, outgoing)
     def to_x(s):
         return gx + 1 < NGX if s else gx > 0
 
@@ -284,6 +281,9 @@
     across(0).start()
     start_halos(0)
     each(1, 5, lambda q: near_gather(q, 0).start())
+    loads[3].wait()
+    loads[6].wait()
+    each(0, 4, outgoing)
 
     loads[4].wait()
     jm = lane_i(256)
@@ -473,18 +473,21 @@
     p = pressure[...]
     high = p.astype(BF16)
     low = (p - high.astype(F32)).astype(BF16)
+    m = pmap[...]
+    mult_force = lift * tn(reaction[...], m)
+    res_force = lift * tn(jnp.concatenate([high, low]), jnp.concatenate([m, m]))
     copies = []
     for b in range(4):
         at = (b // 2, b % 2)
-        m = pmap[:, b * 128:(b + 1) * 128]
-        mult = mult_in[at] + lift * tn(reaction[...], m)
-        mult_v[at] = mult
-        copies.append(pltpu.make_async_copy(mult_v.at[at], mult_h.at[at], sem.at[0, b]))
-        copies[-1].start()
-        res_v[at] = res_in[at] + lift * (tn(high, m) + tn(low, m))
-        copies.append(pltpu.make_async_copy(res_v.at[at], res_h.at[at], sem.at[1, b]))
-        copies[-1].start()
-        sens_o[at] = jnp.sum(mult * own[at]) * scale
+        lanes = slice(b * 128, (b + 1) * 128)
+        for i, (force, src, buf, out) in enumerate((
+                (mult_force, mult_in, mult_v, mult_h), (res_force, res_in, res_v, res_h))):
+            buf[at] = src[at] + force[:, lanes]
+            copies.append(pltpu.make_async_copy(buf.at[at], out.at[at], sem.at[i, b]))
+            copies[-1].start()
+    for b in range(4):
+        at = (b // 2, b % 2)
+        sens_o[at] = jnp.sum(mult_v[at] * own[at]) * scale
     for c in copies:
         c.wait()
 

time: 48.3 us -> 48.3 us (level)
  no operation moved by 1% of the time
where the time goes in v5:
time: 48.3 us; the launch traced here: 48.2 us
  Pallas kernels  47.5 us (98%)
  between operations  0.64 us (1%)
    pallas_call x1, Pallas kernels, on_device(): pl.pallas_call(kernel, out_shape=(whole, whole, whole, jax.ShapeDtypeStru...  45.7 us
    pallas_call x1, Pallas kernels, on_device(): pl.pallas_call(functools.partial(finish, lift, 1.0 / 128.0), out_shape=(w...  1.89 us

profile of v5, /device:TPU:1, one launch (start us, length us, event | category | flops | bytes accessed | tf_op | source)
XLA Modules:
  0.0 48.2 jit_solution(2540017618837675314)
XLA Ops:
  0.6 45.7 %plate.1 = (f32[2,2,256,128]{3,2,1,0:T(8,128)S(1)}, f32[2,2,256,128]{3,2,1,0:T(8,128)S(1)}, f32[2,2,256,128]{3,2,1,0:T(8,128)S(1)}, f32[32,256]{1,0:T(8,128)S(1)...) custom-call(s32[2,2,4]{2,1,0:T(2,128)} %joints_h.1, bf16[2,2,256,128]{3,2,1,0:T(8,128)(2,1)} %bitcast.8, ...), custom_call_target="tpu_custom_call" | custom-call | tf_op jit(solution)/shard_map/plate/pallas_call | solution.py:504
  46.3 1.9 %finish.1 = (f32[2,2,256,128]{3,2,1,0:T(8,128)}, f32[2,2,256,128]{3,2,1,0:T(8,128)}, f32[2,2]{1,0:T(2,128)}) custom-call(f32[32,256]{1,0:T(8,128)S(1)} %get-tuple-element.12.pressure, bf16[32,256]{1,0:T(8,128)(2,1)S(1)} %get-tuple-element.13.reaction, bf16[32,512]{1,0:T(8,128)(2,1)S(1)} %get-tuple-element.14.pmap, ...), custom_call_target="tpu_custom_call" | custom-call | tf_op jit(solution)/shard_map/finish/pallas_call | solution.py:568
